TPU v7x, 32 devices: a whole 2x2x4 slice. The times are simulated.
32 devices in a mesh: ctx: 8 (over y, x, core), chan: 4 (over z).
Axes of the slice: x: 2, y: 2, z: 4, core: 2. Of those that a mesh axis runs over, the one named last changes fastest.
Arguments:
- x_gate: bfloat16 [1024, 4096], P('ctx', 'chan'), may hold values from -6 to 6
- x_key: bfloat16 [1024, 4096], P('ctx', 'chan'), may hold values from -6 to 6
- x_value: bfloat16 [1024, 4096], P('ctx', 'chan'), may hold values from -6 to 6
- filters: bfloat16 [1024, 256], P('ctx', 'chan'), may hold values from -1.1 to 1.1
- bias: float32 [4096], P('chan'), may hold values from 0.5 to 1.5
- w_out: bfloat16 [4096, 4096], P('chan'), may hold values from -0.09375 to 0.09375
Outputs:
- mixed: bfloat16 [1024, 4096], P('ctx', 'chan')
All inputs are finite; a program needn't handle non-finite values.
Results may differ from a plain program's by a relative error of at most 0.014.
Values may be sent and summed in bfloat16 or wider, within the bound.
No kernel may reach another device: no remote copies, remote signals or barrier semaphores. Data moves between devices by JAX's collectives and lax.ppermute only.
A program may use at most 64 MiB of HBM per device.

v0:
```python
import jax
import jax.numpy as jnp
from jax import lax
from jax.sharding import PartitionSpec as P


def block_product(padded_taps, groups, lag, source):
    rows = source.shape[0]
    total_len = padded_taps.shape[0] // 2
    span = 2 * rows - 1
    window = lax.dynamic_slice_in_dim(padded_taps, total_len + lag - (rows - 1), span, 0)
    flipped = window[::-1]
    tiled = jnp.tile(flipped, (rows, 1))
    toeplitz = tiled[rows - 1 : rows - 1 + rows * (span - 1)].reshape(rows, span - 1, groups)[
        :, :rows
    ]
    shaped = source.reshape(rows, groups, source.shape[1] // groups)
    result = jnp.einsum("tsg,sgc->tgc", toeplitz, shaped, preferred_element_type=jnp.float32)
    return result.reshape(rows, source.shape[1])


def local(x_gate, x_key, x_value, filters, bias, w_out):
    tok_rows = x_key.shape[0]
    groups = filters.shape[1]
    z = (x_key.astype(jnp.float32) * x_value.astype(jnp.float32)).astype(jnp.bfloat16)
    all_taps = lax.all_gather(filters, "ctx", axis=0, tiled=True)
    total_len = all_taps.shape[0]
    blocks = lax.axis_size("ctx")
    slab_groups = groups // blocks
    column = lax.all_to_all(z, "ctx", split_axis=1, concat_axis=0, tiled=True)
    own_taps = lax.dynamic_slice_in_dim(
        all_taps, lax.axis_index("ctx") * slab_groups, slab_groups, 1
    )
    padded = jnp.concatenate([jnp.zeros_like(own_taps), own_taps], axis=0)
    slab_width = column.shape[1]

    def one_block(block):

        def add_source(src, total):
            source = lax.dynamic_slice_in_dim(column, src * tok_rows, tok_rows, 0)
            return total + block_product(padded, slab_groups, (block - src) * tok_rows, source)

        return lax.fori_loop(
            0, block + 1, add_source, jnp.zeros((tok_rows, slab_width), jnp.float32)
        )

    pieces = lax.map(one_block, jnp.arange(blocks, dtype=jnp.int32))
    whole_conv = pieces.reshape(total_len, slab_width)
    conv = lax.all_to_all(
        whole_conv.astype(jnp.bfloat16), "ctx", split_axis=0, concat_axis=1, tiled=True
    ).astype(whole_conv.dtype)
    gated = (x_gate.astype(jnp.float32) * (conv + bias[None, :] * z.astype(jnp.float32))).astype(
        jnp.bfloat16
    )
    summed = lax.psum_scatter(
        lax.dot_general(
            w_out, gated, (((0,), (1,)), ((), ())), preferred_element_type=jnp.float32
        ).astype(jnp.bfloat16),
        "chan",
        scatter_dimension=0,
        tiled=True,
    ).astype(jnp.float32)
    return summed.T.astype(jnp.bfloat16)


def solution(mesh):
    placed = (
        P("ctx", "chan"),
        P("ctx", "chan"),
        P("ctx", "chan"),
        P("ctx", "chan"),
        P("chan"),
        P("chan", None),
    )
    return jax.shard_map(
        local, mesh=mesh, in_specs=placed, out_specs=P("ctx", "chan"), check_vma=False
    )
```

profile of v0, /device:TPU:0, one launch (start us, length us, event | category | flops | bytes accessed | tf_op | source)
XLA Modules:
  0.0 227.2 jit_solution(1479955118835113915)
XLA Ops:
  8.5 5.2 %all-to-all-start = ((bf16[128,8,128]{0,2,1:T(8,128)(2,1)}), bf16[128,8,128]{0,2,1:T(8,128)(2,1)S(1)}, u32[]{:S(2)}, u32[]{:S(2)}) async-start(bf16[128,8,128]{0,2,1:T(8,128)(2,1)} %bitcast.5), calls=%async_computation | async-start | bytes 524288 | tf_op jit(solution)/shard_map/all_to_all | solution.py:30
  13.7 10.2 %all_gather.3 = bf16[1024,64]{0,1:T(8,128)(2,1)S(1)} all-gather(bf16[128,64]{0,1:T(8,128)(2,1)} %param.13), channel_id=1, replica_groups=mesh['ctx'=8,'chan'=4] {'ctx'}, dimensions={0}, use_global_device_ids=true | all-gather | bytes 147456 | tf_op jit(solution)/shard_map/all_gather | solution.py:26
  24.3 153.8 %while.41 = (s32[]{:T(128)}, bf16[8,128,128]{1,2,0:T(8,128)(2,1)S(1)}, s32[8]{0:T(128)S(1)}, bf16[1024,128]{0,1:T(8,128)(2,1)S(1)}, bf16[2048,8]{0,1:T(8,128)(2,...) while((s32[]{:T(128)}, ...), condition=%wide.region_3.4_spmd, body=%wide.region_0.3_spmd.sunk | while | flops 4210703 | bytes 4495790 | solution.py:47
  25.7 4.0 %while.42 = (s32[]{:T(128)}, f32[128,128]{0,1:T(8,128)S(1)}, s32[]{:T(128)}, bf16[1024,128]{0,1:T(8,128)(2,1)S(1)}, s32[]{:T(128)}, /*index=5*/bf16[2048,8]{0,1:...) while((s32[]{:T(128)}, f32[128,128]{0,1:T(8,128)S(1)}, ...), condition=%wide.region_2.2_spmd, body=%wide.region_1.1_spmd.sunk | while | flops 4210700 | bytes 4298913 | solution.py:43
  27.6 1.7 reshape.40
  31.1 7.9 %while.42 = (s32[]{:T(128)}, f32[128,128]{0,1:T(8,128)S(1)}, s32[]{:T(128)}, bf16[1024,128]{0,1:T(8,128)(2,1)S(1)}, s32[]{:T(128)}, /*index=5*/bf16[2048,8]{0,1:...) while((s32[]{:T(128)}, f32[128,128]{0,1:T(8,128)S(1)}, ...), condition=%wide.region_2.2_spmd, body=%wide.region_1.1_spmd.sunk | while | flops 4210700 | bytes 4298913 | solution.py:43
  40.4 11.9 %while.42 = (s32[]{:T(128)}, f32[128,128]{0,1:T(8,128)S(1)}, s32[]{:T(128)}, bf16[1024,128]{0,1:T(8,128)(2,1)S(1)}, s32[]{:T(128)}, /*index=5*/bf16[2048,8]{0,1:...) while((s32[]{:T(128)}, f32[128,128]{0,1:T(8,128)S(1)}, ...), condition=%wide.region_2.2_spmd, body=%wide.region_1.1_spmd.sunk | while | flops 4210700 | bytes 4298913 | solution.py:43
  42.3 1.7 reshape.40
  46.3 1.7 reshape.40
  53.7 15.8 %while.42 = (s32[]{:T(128)}, f32[128,128]{0,1:T(8,128)S(1)}, s32[]{:T(128)}, bf16[1024,128]{0,1:T(8,128)(2,1)S(1)}, s32[]{:T(128)}, /*index=5*/bf16[2048,8]{0,1:...) while((s32[]{:T(128)}, f32[128,128]{0,1:T(8,128)S(1)}, ...), condition=%wide.region_2.2_spmd, body=%wide.region_1.1_spmd.sunk | while | flops 4210700 | bytes 4298913 | solution.py:43
  55.6 1.7 reshape.40
  59.6 1.7 reshape.40
  70.9 19.8 %while.42 = (s32[]{:T(128)}, f32[128,128]{0,1:T(8,128)S(1)}, s32[]{:T(128)}, bf16[1024,128]{0,1:T(8,128)(2,1)S(1)}, s32[]{:T(128)}, /*index=5*/bf16[2048,8]{0,1:...) while((s32[]{:T(128)}, f32[128,128]{0,1:T(8,128)S(1)}, ...), condition=%wide.region_2.2_spmd, body=%wide.region_1.1_spmd.sunk | while | flops 4210700 | bytes 4298913 | solution.py:43
  72.9 1.7 reshape.40
  76.9 1.7 reshape.40
  84.8 1.7 reshape.40
  88.7 1.7 reshape.40
  92.2 23.7 %while.42 = (s32[]{:T(128)}, f32[128,128]{0,1:T(8,128)S(1)}, s32[]{:T(128)}, bf16[1024,128]{0,1:T(8,128)(2,1)S(1)}, s32[]{:T(128)}, /*index=5*/bf16[2048,8]{0,1:...) while((s32[]{:T(128)}, f32[128,128]{0,1:T(8,128)S(1)}, ...), condition=%wide.region_2.2_spmd, body=%wide.region_1.1_spmd.sunk | while | flops 4210700 | bytes 4298913 | solution.py:43
  102.0 1.7 reshape.40
  117.3 27.7 %while.42 = (s32[]{:T(128)}, f32[128,128]{0,1:T(8,128)S(1)}, s32[]{:T(128)}, bf16[1024,128]{0,1:T(8,128)(2,1)S(1)}, s32[]{:T(128)}, /*index=5*/bf16[2048,8]{0,1:...) while((s32[]{:T(128)}, f32[128,128]{0,1:T(8,128)S(1)}, ...), condition=%wide.region_2.2_spmd, body=%wide.region_1.1_spmd.sunk | while | flops 4210700 | bytes 4298913 | solution.py:43
  146.4 31.7 %while.42 = (s32[]{:T(128)}, f32[128,128]{0,1:T(8,128)S(1)}, s32[]{:T(128)}, bf16[1024,128]{0,1:T(8,128)(2,1)S(1)}, s32[]{:T(128)}, /*index=5*/bf16[2048,8]{0,1:...) while((s32[]{:T(128)}, f32[128,128]{0,1:T(8,128)S(1)}, ...), condition=%wide.region_2.2_spmd, body=%wide.region_1.1_spmd.sunk | while | flops 4210700 | bytes 4298913 | solution.py:43
  178.1 9.4 %all_to_all.29 = bf16[8,128,128]{1,2,0:T(8,128)(2,1)S(1)} all-to-all(bf16[8,128,128]{1,2,0:T(8,128)(2,1)S(1)} %get-tuple-element.251), channel_id=1, replica_groups=mesh['ctx'=8,'chan'=4] {'ctx'}, dimensions={0} | all-to-all | bytes 524288 | tf_op jit(solution)/shard_map/all_to_all | solution.py:49
  187.8 5.7 %fusion.2 = bf16[4096,128]{0,1:T(8,128)(2,1)} fusion(bf16[1024,4096]{1,0:T(8,128)(2,1)} %param.15, f32[128,1024]{1,0:T(8,128)S(1)} %copy.16, bf16[128,1024]{1,0:T(8,128)(2,1)S(1)} %multiply_convert_fusion.1, bf16[128,1024]{1,0:T(8,128)(2,1)S(1)} %copy-done, f32[1024]{0:T(1024)S(1)} %copy-done.1), kind=kOutput, calls=%fused_computation.7 | convolution fusion | flops 1075052544 | bytes 10489856 | tf_op jit(solution)/shard_map/dot_general | solution.py:56
  193.5 26.8 %reduce-scatter.2.cloned.1.call-done = bf16[1024,128]{0,1:T(8,128)(2,1)} async-done(((bf16[4096,128]{0,1:T(8,128)(2,1)}), bf16[1024,128]{0,1:T(8,128)(2,1)}) %reduce-scatter.2.cloned.1.call-update) | async-done | bytes 262160 | tf_op jit(solution)/shard_map/reduce_scatter | solution.py:55
  (391 shorter events, 106.2 us)
Async XLA Ops:
  8.5 15.4 %all-to-all-start = ((bf16[128,8,128]{0,2,1:T(8,128)(2,1)}), bf16[128,8,128]{0,2,1:T(8,128)(2,1)S(1)}, u32[]{:S(2)}, u32[]{:S(2)}) async-start(bf16[128,8,128]{0,2,1:T(8,128)(2,1)} %bitcast.5), calls=%async_computation | async-start | bytes 524288 | tf_op jit(solution)/shard_map/all_to_all | solution.py:30
  13.7 206.7 %reduce-scatter.2.cloned.1.call-start = ((), (), s32[]{:S(2)}) async-start(), calls=%async_computation.3 | async-start | bytes 1310720 | tf_op jit(solution)/shard_map/reduce_scatter | solution.py:55
  24.3 163.6 %copy-start = (bf16[128,1024]{1,0:T(8,128)(2,1)S(1)}, bf16[128,1024]{1,0:T(8,128)(2,1)}, u32[]{:S(2)}) copy-start(bf16[128,1024]{1,0:T(8,128)(2,1)} %param.10) | copy-start | bytes 786436
  24.3 163.6 %copy-start.1 = (f32[1024]{0:T(1024)S(1)}, f32[1024]{0:T(1024)}, u32[]{:S(2)}) copy-start(f32[1024]{0:T(1024)} %param.14) | copy-start | bytes 12292
Sparse Core Ops, SparseCore 0:
  193.7 26.6 reduce-scatter.1
where the time goes:
time: 228 us; the launch traced here: 227 us
  local copies, waits for them, and re-layouts  113 us (50%)
  loops' own time  33.2 us (15%)
  waiting for transfers between devices  26.8 us (12%)
  blocking collectives  19.6 us (9%)
  matrix products  14.1 us (6%)
  between operations  13.5 us (6%)
  starting transfers between devices  5.23 us (2%)
    reshape x36, local copies, waits for them, and re-layouts, block_product(): tiled[rows - 1:rows - 1 + rows * (span - 1)].reshape(rows, span - 1, groups)  61.2 us
    another operation x8, loops' own time, one_block(): lax.fori_loop(0, block + 1, add_source, jnp.zeros((tok_rows, slab_width),...  27.4 us
    reduce_scatter x1, waiting for transfers between devices, local(): lax.psum_scatter(lax.dot_general(w_out, gated, (((0,), (1,)), ((), ())),...  26.8 us
    another operation x72, local copies, waits for them, and re-layouts, block_product(): tiled = jnp.tile(flipped, (rows, 1))  24.8 us
    all_gather x1, blocking collectives, local(): all_taps = lax.all_gather(filters, 'ctx', axis=0, tiled=True)  10.2 us
    all_to_all x1, blocking collectives, local(): lax.all_to_all(whole_conv.astype(jnp.bfloat16), 'ctx', split_axis=0, conc...  9.44 us
    while x72, local copies, waits for them, and re-layouts  8.68 us
    dot_general x36, matrix products, block_product(): jnp.einsum('tsg,sgc->tgc', toeplitz, shaped, preferred_element_type=jnp.f...  8.41 us
  transfers between devices with their start and end apart: 2, of which 1 were waited for; matrix products, arithmetic and copies ran while one was open for 0% of the time, Pallas kernels for 0%

commit v1 on v0

v1 whole, which is shorter than its diff:
```python
import functools

import jax
import jax.numpy as jnp
from jax import lax
from jax.experimental import pallas as pl
from jax.experimental.pallas import tpu as pltpu
from jax.sharding import PartitionSpec as P

F32 = jnp.float32
BF16 = jnp.bfloat16


def pad_rows(rows):
    return -(-rows // 16) * 16


def pack_kernel(parts, key_ref, value_ref, taps_ref, out_ref):
    channels = key_ref.shape[1] // parts
    groups = taps_ref.shape[0] // parts
    tokens = key_ref.shape[0]
    taps = taps_ref[...].astype(F32)
    filler = jnp.zeros((pad_rows(groups) - groups, tokens), F32)
    for part in range(parts):
        lanes = slice(part * channels, (part + 1) * channels)
        z = (key_ref[:, lanes].astype(F32) * value_ref[:, lanes].astype(F32)).astype(BF16)
        out_ref[part, :channels, :] = z.T
        mine = taps[part * groups : (part + 1) * groups]
        if filler.shape[0]:
            mine = jnp.concatenate([mine, filler], axis=0)
        out_ref[part, channels:, :] = mine.astype(BF16)


def pack(x_key, x_value, taps, parts):
    tokens, width = x_key.shape
    rows = width // parts + pad_rows(taps.shape[0] // parts)
    return pl.pallas_call(
        functools.partial(pack_kernel, parts),
        out_shape=jax.ShapeDtypeStruct((parts, rows, tokens), BF16),
        name="pack",
    )(x_key, x_value, taps)


def conv_kernel(size, groups, in_ref, out_ref):
    blocks, _, tokens = in_ref.shape
    channels = size * groups
    row = lax.broadcasted_iota(jnp.int32, (tokens, tokens), 0)
    col = lax.broadcasted_iota(jnp.int32, (tokens, tokens), 1)
    later = col >= row
    for group in range(groups):
        tiles = []
        before = jnp.zeros((tokens, tokens), F32)
        for block in range(blocks):
            taps = in_ref[block, channels + group : channels + group + 1, :].astype(F32)
            spread = jnp.broadcast_to(taps, (tokens, tokens))
            rolled = pltpu.roll(spread, 0, 1, stride=1, stride_axis=0)
            tiles.append(jnp.where(later, rolled, before).astype(BF16))
            before = rolled
        toeplitz = jnp.concatenate(tiles, axis=1)
        source = in_ref[:, group * size : (group + 1) * size, :].reshape(blocks * size, tokens)
        product = jnp.dot(source, toeplitz, preferred_element_type=F32)
        for block in range(blocks):
            total = product[:size, block * tokens : (block + 1) * tokens]
            for src in range(1, block + 1):
                lag = block - src
                total = total + product[
                    src * size : (src + 1) * size, lag * tokens : (lag + 1) * tokens
                ]
            out_ref[block, group * size : (group + 1) * size, :] = total.astype(BF16)


def conv(received, size, groups):
    blocks, _, tokens = received.shape
    return pl.pallas_call(
        functools.partial(conv_kernel, size, groups),
        out_shape=jax.ShapeDtypeStruct((blocks, size * groups, tokens), BF16),
        name="conv",
    )(received)


def gate_kernel(which_ref, conv_ref, gate_ref, key_ref, value_ref, bias_ref, w_ref, gated_ref, part_ref):
    parts, channels, _ = conv_ref.shape
    for part in range(parts):
        lanes = slice(part * channels, (part + 1) * channels)
        z = (key_ref[:, lanes].astype(F32) * value_ref[:, lanes].astype(F32)).astype(BF16)
        mixed = conv_ref[part].T.astype(F32) + bias_ref[:, lanes] * z.astype(F32)
        gated_ref[:, lanes] = (gate_ref[:, lanes].astype(F32) * mixed).astype(BF16)
    part_ref[...] = jnp.dot(gated_ref[...], w_ref[...], preferred_element_type=F32).astype(BF16)


def gate_and_project(which, conved, x_gate, x_key, x_value, bias, w_out, width):
    tokens, depth = x_gate.shape
    full = lambda shape: pl.BlockSpec(shape, lambda i, which: (0,) * len(shape))
    grid_spec = pltpu.PrefetchScalarGridSpec(
        num_scalar_prefetch=1,
        grid=(1,),
        in_specs=[
            full(conved.shape),
            full(x_gate.shape),
            full(x_key.shape),
            full(x_value.shape),
            full((1, depth)),
            pl.BlockSpec((depth, width), lambda i, which: (0, which[0])),
        ],
        out_specs=[full((tokens, depth)), full((tokens, width))],
    )
    return pl.pallas_call(
        gate_kernel,
        grid_spec=grid_spec,
        out_shape=[
            jax.ShapeDtypeStruct((tokens, depth), BF16),
            jax.ShapeDtypeStruct((tokens, width), BF16),
        ],
        name="gate",
    )(which, conved, x_gate, x_key, x_value, bias.reshape(1, depth), w_out)


def project_kernel(which_ref, gated_ref, w_ref, part_ref):
    part_ref[0] = jnp.dot(gated_ref[...], w_ref[...], preferred_element_type=F32).astype(BF16)


def project(which, gated, w_out, width):
    tokens, depth = gated.shape
    steps = which.shape[0]
    grid_spec = pltpu.PrefetchScalarGridSpec(
        num_scalar_prefetch=1,
        grid=(steps,),
        in_specs=[
            pl.BlockSpec((tokens, depth), lambda i, which: (0, 0)),
            pl.BlockSpec((depth, width), lambda i, which: (0, which[i])),
        ],
        out_specs=pl.BlockSpec((1, tokens, width), lambda i, which: (i, 0, 0)),
    )
    return pl.pallas_call(
        project_kernel,
        grid_spec=grid_spec,
        out_shape=jax.ShapeDtypeStruct((steps, tokens, width), BF16),
        name="project",
    )(which, gated, w_out)


def local(x_gate, x_key, x_value, filters, bias, w_out):
    tokens, depth = x_key.shape
    parts = lax.axis_size("ctx")
    planes = lax.axis_size("chan")
    width = w_out.shape[1] // planes
    size = depth // filters.shape[1]
    groups = filters.shape[1] // parts

    sent = pack(x_key, x_value, filters.T, parts)
    received = lax.all_to_all(sent, "ctx", split_axis=0, concat_axis=0, tiled=True)
    conved = conv(received, size, groups)
    conved = lax.all_to_all(conved, "ctx", split_axis=0, concat_axis=0, tiled=True)

    me = lax.axis_index("chan")
    if planes != 4:
        gated, first = gate_and_project(
            jnp.zeros((1,), jnp.int32), conved, x_gate, x_key, x_value, bias, w_out, width
        )
        rest = project(jnp.arange(1, planes, dtype=jnp.int32), gated, w_out, width)
        whole = jnp.concatenate([first[None], rest], axis=0)
        return lax.psum_scatter(whole, "chan", scatter_dimension=0, tiled=False)

    inner = (me == 1) | (me == 2)
    order = jnp.array([[3, 2, 1, 0], [0, 2, 3, 1], [3, 1, 0, 2], [0, 1, 2, 3]], jnp.int32)
    order = lax.dynamic_index_in_dim(order, me, 0, keepdims=False)
    gated, near = gate_and_project(
        order[:1], conved, x_gate, x_key, x_value, bias, w_out, width
    )
    from_near = lax.ppermute(near, "chan", [(0, 1), (1, 0), (2, 3), (3, 2)])
    second = project(order[1:2], gated, w_out, width)[0]
    from_middle = lax.ppermute(second, "chan", [(1, 2), (2, 1)])
    from_far = lax.ppermute(second, "chan", [(0, 2), (3, 1)])
    last = project(order[2:], gated, w_out, width)
    relay = (last[0].astype(F32) + jnp.where(inner, from_near.astype(F32), 0.0)).astype(BF16)
    from_relay = lax.ppermute(relay, "chan", [(0, 1), (1, 3), (3, 2), (2, 0)])
    total = last[1].astype(F32) + jnp.where(inner, 0.0, from_near.astype(F32))
    total = total + from_middle.astype(F32) + from_far.astype(F32) + from_relay.astype(F32)
    return total.astype(BF16)


def solution(mesh):
    placed = (
        P("ctx", "chan"),
        P("ctx", "chan"),
        P("ctx", "chan"),
        P("ctx", "chan"),
        P("chan"),
        P("chan", None),
    )
    return jax.shard_map(
        local, mesh=mesh, in_specs=placed, out_specs=P("ctx", "chan"), check_vma=False
    )
```

time: 228 us -> 61.2 us (0.27)
  local copies, waits for them, and re-layouts: 113 us -> 2.65 us
  loops' own time: 33.2 us -> 0 us
  Pallas kernels: 0 us -> 15.9 us
  matrix products: 14.1 us -> 0 us
  between operations: 13.5 us -> 0.04 us
  waiting for transfers between devices: 26.8 us -> 15 us
  blocking collectives: 19.6 us -> 12.6 us
  starting transfers between devices: 5.23 us -> 11.6 us
    reshape x36 -> x0, local copies, waits for them, and re-layouts: 61.2 us -> none  [block_product(): tiled[rows - 1:rows - 1 + rows * (span - 1)].reshape(rows, span - 1, groups)]
    another operation x9 -> x0, loops' own time: 33.2 us -> none  [the longest x8 27.4 us: one_block(): lax.fori_loop(0, block + 1, add_source, jnp.zeros((tok_rows, slab_width),...]
    reduce_scatter x1 -> x0, waiting for transfers between devices: 26.8 us -> none  [local(): lax.psum_scatter(lax.dot_general(w_out, gated, (((0,), (1,)), ((), ())),...]
    another operation x80 -> x0, local copies, waits for them, and re-layouts: 24.8 us -> none  [the longest x72 24.8 us: block_product(): tiled = jnp.tile(flipped, (rows, 1))]
    pallas_call x0 -> x5, Pallas kernels: none -> 15.9 us  [the longest x2 7.69 us: project(): pl.pallas_call(project_kernel, grid_spec=grid_spec, out_shape=jax.ShapeDt...]
    dot_general x37 -> x0, matrix products: 14.1 us -> none  [the longest x36 8.41 us: block_product(): jnp.einsum('tsg,sgc->tgc', toeplitz, shaped, preferred_element_type=jnp.f...]
    all_gather x1 -> x0, blocking collectives: 10.2 us -> none  [local(): all_taps = lax.all_gather(filters, 'ctx', axis=0, tiled=True)]
    ppermute x0 -> x4, waiting for transfers between devices: none -> 9.53 us  [the longest x1 9.53 us: local(): from_relay = lax.ppermute(relay, 'chan', [(0, 1), (1, 3), (3, 2), (2, 0)])]
  transfers between devices with their start and end apart: 2 -> 5, of which waited for: 1 -> 2; matrix products, arithmetic and copies ran while one was open for 0% -> 5% of each run, Pallas kernels for 0% -> 13%
where the time goes in v1:
time: 61.2 us; the launch traced here: 60.7 us
  Pallas kernels  15.9 us (26%)
  waiting for transfers between devices  15 us (25%)
  blocking collectives  12.6 us (21%)
  starting transfers between devices  11.6 us (19%)
  other arithmetic  2.92 us (5%)
  local copies, waits for them, and re-layouts  2.65 us (4%)
    all_to_all x1, blocking collectives, local(): lax.all_to_all(sent, 'ctx', split_axis=0, concat_axis=0, tiled=True)  12.6 us
    ppermute x1, waiting for transfers between devices, local(): from_relay = lax.ppermute(relay, 'chan', [(0, 1), (1, 3), (3, 2), (2, 0)])  9.53 us
    pallas_call x2, Pallas kernels, project(): pl.pallas_call(project_kernel, grid_spec=grid_spec, out_shape=jax.ShapeDt...  7.69 us
    all_to_all x1, waiting for transfers between devices, local(): lax.all_to_all(conved, 'ctx', split_axis=0, concat_axis=0, tiled=True)  5.49 us
    ppermute x1, starting transfers between devices, local(): from_far = lax.ppermute(second, 'chan', [(0, 2), (3, 1)])  4.5 us
    pallas_call x1, Pallas kernels, gate_and_project(): pl.pallas_call(gate_kernel, grid_spec=grid_spec, out_shape=[jax.ShapeDtyp...  3.86 us
    all_to_all x1, starting transfers between devices, local(): lax.all_to_all(conved, 'ctx', split_axis=0, concat_axis=0, tiled=True)  3.41 us
    pallas_call x1, Pallas kernels, conv(): pl.pallas_call(functools.partial(conv_kernel, size, groups), out_shape=ja...  2.44 us
  transfers between devices with their start and end apart: 5, of which 2 were waited for; matrix products, arithmetic and copies ran while one was open for 5% of the time, Pallas kernels for 13%

profile of v1, /device:TPU:0, one launch (start us, length us, event | category | flops | bytes accessed | tf_op | source)
XLA Modules:
  0.0 60.7 jit_solution(367314421506714944)
XLA Ops:
  0.0 1.9 %pack.1 = bf16[8,144,128]{2,1,0:T(8,128)(2,1)} custom-call(bf16[128,1024]{1,0:T(8,128)(2,1)} %key_ref.3, bf16[128,1024]{1,0:T(8,128)(2,1)} %value_ref.3, bf16[64,128]{1,0:T(8,128)(2,1)} %bitcast.19), custom_call_target="tpu_custom_call" | custom-call | tf_op jit(solution)/shard_map/pack/pallas_call | solution.py:37
  1.9 12.6 %all_to_all.10.in_ref = bf16[8,144,128]{2,1,0:T(8,128)(2,1)} all-to-all(bf16[8,144,128]{2,1,0:T(8,128)(2,1)} %pack.1), channel_id=1, replica_groups=mesh['ctx'=8,'chan'=4] {'ctx'}, dimensions={0} | all-to-all | bytes 589824 | tf_op jit(solution)/shard_map/all_to_all | solution.py:151
  14.4 2.4 %conv.1 = bf16[8,128,128]{2,1,0:T(8,128)(2,1)} custom-call(bf16[8,144,128]{2,1,0:T(8,128)(2,1)} %all_to_all.10.in_ref), custom_call_target="tpu_custom_call" | custom-call | tf_op jit(solution)/shard_map/conv/pallas_call | solution.py:74
  16.9 3.4 %all-to-all-start.1 = ((bf16[8,128,128]{2,1,0:T(8,128)(2,1)}), bf16[8,128,128]{2,1,0:T(8,128)(2,1)S(1)}, u32[]{:S(2)}, u32[]{:S(2)}) async-start(bf16[8,128,128]{2,1,0:T(8,128)(2,1)} %conv.1), calls=%async_computation.1 | async-start | bytes 524288 | tf_op jit(solution)/shard_map/all_to_all | solution.py:153
  20.3 0.7 %constant_dynamic-slice_fusion = s32[1,4]{1,0:T(1,128)S(1)} fusion(s32[4,4]{1,0:T(4,128)} %constant.18.clone, s32[]{:T(128)S(6)} %select_n.18), kind=kLoop, calls=%fused_computation.12 | loop fusion | bytes 36 | tf_op jit(solution)/shard_map/jit(dynamic_index_in_dim)/dynamic_slice | solution.py:166
  21.0 0.7 %fusion.7 = (s32[1,1]{1,0:T(1,128)}, s32[1,1]{1,0:T(1,128)}) fusion(s32[1,4]{1,0:T(1,128)S(1)} %constant_dynamic-slice_fusion), kind=kLoop, calls=%fused_computation.13 | loop fusion | bytes 16 | tf_op jit(solution)/shard_map/slice | solution.py:171
  21.6 5.5 %all-to-all-done.1.conv_ref = bf16[8,128,128]{2,1,0:T(8,128)(2,1)S(1)} async-done(((bf16[8,128,128]{2,1,0:T(8,128)(2,1)}), bf16[8,128,128]{2,1,0:T(8,128)(2,1)S(1)}, u32[]{:S(2)}, u32[]{:S(2)}) %all-to-all-start.1) | async-done | bytes 262176 | tf_op jit(solution)/shard_map/all_to_all | solution.py:153
  27.1 0.0 copy-start
  27.1 0.7 %copy-done = bf16[8,128,128]{2,1,0:T(8,128)(2,1)} copy-done((bf16[8,128,128]{2,1,0:T(8,128)(2,1)}, bf16[8,128,128]{2,1,0:T(8,128)(2,1)S(1)}, u32[]{:S(2)}) %copy-start) | copy-done | bytes 262168
  27.8 3.9 %gate.1 = (bf16[128,1024]{1,0:T(8,128)(2,1)}, bf16[128,1024]{1,0:T(8,128)(2,1)}) custom-call(s32[1]{0:T(128)} %bitcast.1.which_ref, bf16[8,128,128]{2,1,0:T(8,128)(2,1)} %copy-done, bf16[128,1024]{1,0:T(8,128)(2,1)} %gate_ref.1, bf16[128,1024]{1,0:T(8,128)(2,1)} %key_ref.3, bf16[128,1024]{1,0:T(8,128)(2,1)} %value_ref.3, f32[1,1024]{1,0:T(1,128)} %bitcast.20, ...), custom_call_target="tpu_custom_call" | custom-call | tf_op jit(solution)/shard_map/gate/pallas_call | solution.py:107
  31.7 1.8 %collective-permute-start = (bf16[128,1024]{1,0:T(8,128)(2,1)}, bf16[128,1024]{1,0:T(8,128)(2,1)S(1)}, u32[]{:S(2)}, u32[]{:S(2)}) collective-permute-start(bf16[128,1024]{1,0:T(8,128)(2,1)} %get-tuple-element.8), channel_id=1, source_target_pairs={{0,1},{1,0},{2,3},{3,2},{4,5},{5,4},{6,7},{7,6},{8,9},{9,8},{10,11... | collective-permute-start | bytes 786440 | tf_op jit(solution)/shard_map/ppermute | solution.py:170
  33.5 0.6 slice_bitcast_fusion.2.which_ref
  34.1 3.5 %project.3 = bf16[1,128,1024]{2,1,0:T(8,128)(2,1)} custom-call(s32[1]{0:T(128)} %bitcast.5.which_ref, bf16[128,1024]{1,0:T(8,128)(2,1)} %get-tuple-element.7.gated_ref, bf16[1024,4096]{1,0:T(8,128)(2,1)} %w_ref.5), custom_call_target="tpu_custom_call" | custom-call | tf_op jit(solution)/shard_map/project/pallas_call | solution.py:134
  37.6 4.5 %collective-permute-start.2 = (bf16[128,1024]{1,0:T(8,128)(2,1)}, bf16[128,1024]{1,0:T(8,128)(2,1)S(1)}, u32[]{:S(2)}, u32[]{:S(2)}) collective-permute-start(bf16[128,1024]{1,0:T(8,128)(2,1)} %bitcast.17), channel_id=1, source_target_pairs={{0,2},{3,1},{4,6},{7,5},{8,10},{11,9},{12,14},{15,13},{16,18},{19,... | collective-permute-start | bytes 786440 | tf_op jit(solution)/shard_map/ppermute | solution.py:173
  42.1 0.7 %collective-permute-start.1 = (bf16[128,1024]{1,0:T(8,128)(2,1)}, bf16[128,1024]{1,0:T(8,128)(2,1)S(1)}, u32[]{:S(2)}, u32[]{:S(2)}) collective-permute-start(bf16[128,1024]{1,0:T(8,128)(2,1)} %bitcast.18), channel_id=1, source_target_pairs={{1,2},{2,1},{5,6},{6,5},{9,10},{10,9},{13,14},{14,13},{17,18},{18,... | collective-permute-start | bytes 786440 | tf_op jit(solution)/shard_map/ppermute | solution.py:172
  42.8 4.2 %project.2 = bf16[2,128,1024]{2,1,0:T(8,128)(2,1)} custom-call(s32[2]{0:T(128)} %slice_bitcast_fusion.2.which_ref, bf16[128,1024]{1,0:T(8,128)(2,1)} %get-tuple-element.7.gated_ref, bf16[1024,4096]{1,0:T(8,128)(2,1)} %w_ref.5), custom_call_target="tpu_custom_call" | custom-call | tf_op jit(solution)/shard_map/project/pallas_call | solution.py:134
  47.0 0.0 collective-permute-done
  47.0 1.0 %fusion.6 = bf16[128,1024]{1,0:T(8,128)(2,1)S(1)} fusion(bf16[128,1024]{1,0:T(8,128)(2,1)S(1)} %collective-permute-done, bf16[2,128,1024]{2,1,0:T(8,128)(2,1)} %project.2, pred[]{:T(512)S(6)} %or.3), kind=kLoop, calls=%fused_computation.8 | loop fusion | flops 655360 | bytes 786433 | tf_op jit(solution)/shard_map/convert_element_type | solution.py:175
  48.0 1.2 %collective-permute-start.3 = (bf16[128,1024]{1,0:T(8,128)(2,1)S(1)}, bf16[128,1024]{1,0:T(8,128)(2,1)S(1)}, u32[]{:S(2)}, u32[]{:S(2)}) collective-permute-start(bf16[128,1024]{1,0:T(8,128)(2,1)S(1)} %fusion.6), channel_id=1, source_target_pairs={{0,1},{1,3},{3,2},{2,0},{4,5},{5,7},{7,6},{6,4},{8,9},{9,11},{11,1... | collective-permute-start | bytes 786440 | tf_op jit(solution)/shard_map/ppermute | solution.py:176
  49.2 0.0 collective-permute-done.2
  49.2 0.0 collective-permute-done.1
  49.2 9.5 %collective-permute-done.3 = bf16[128,1024]{1,0:T(8,128)(2,1)S(1)} collective-permute-done((bf16[128,1024]{1,0:T(8,128)(2,1)S(1)}, bf16[128,1024]{1,0:T(8,128)(2,1)S(1)}, u32[]{:S(2)}, u32[]{:S(2)}) %collective-permute-start.3) | collective-permute-done | bytes 262176 | tf_op jit(solution)/shard_map/ppermute | solution.py:176
  58.8 1.9 %fusion.4 = bf16[128,1024]{1,0:T(8,128)(2,1)} fusion(bf16[128,1024]{1,0:T(8,128)(2,1)S(1)} %collective-permute-done, bf16[128,1024]{1,0:T(8,128)(2,1)S(1)} %collective-permute-done.3, bf16[128,1024]{1,0:T(8,128)(2,1)S(1)} %collective-permute-done.2, bf16[128,1024]{1,0:T(8,128)(2,1)S(1)} %collective-permute-done.1, bf16[2,128,1024]{2,1,0:T(8,128)(2,1)} %project.2, ...), kind=kLoop, calls=%fused_computation.6 | loop fusion | flops 1441792 | bytes 1572865 | tf_op jit(solution)/shard_map/convert_element_type | solution.py:179
Async XLA Ops:
  16.9 10.3 %all-to-all-start.1 = ((bf16[8,128,128]{2,1,0:T(8,128)(2,1)}), bf16[8,128,128]{2,1,0:T(8,128)(2,1)S(1)}, u32[]{:S(2)}, u32[]{:S(2)}) async-start(bf16[8,128,128]{2,1,0:T(8,128)(2,1)} %conv.1), calls=%async_computation.1 | async-start | bytes 524288 | tf_op jit(solution)/shard_map/all_to_all | solution.py:153
  27.1 0.7 %copy-start = (bf16[8,128,128]{2,1,0:T(8,128)(2,1)}, bf16[8,128,128]{2,1,0:T(8,128)(2,1)S(1)}, u32[]{:S(2)}) copy-start(bf16[8,128,128]{2,1,0:T(8,128)(2,1)S(1)} %all-to-all-done.1.conv_ref) | copy-start | bytes 786436
  31.7 15.3 %collective-permute-start = (bf16[128,1024]{1,0:T(8,128)(2,1)}, bf16[128,1024]{1,0:T(8,128)(2,1)S(1)}, u32[]{:S(2)}, u32[]{:S(2)}) collective-permute-start(bf16[128,1024]{1,0:T(8,128)(2,1)} %get-tuple-element.8), channel_id=1, source_target_pairs={{0,1},{1,0},{2,3},{3,2},{4,5},{5,4},{6,7},{7,6},{8,9},{9,8},{10,11... | collective-permute-start | bytes 786440 | tf_op jit(solution)/shard_map/ppermute | solution.py:170
  37.6 11.6 %collective-permute-start.2 = (bf16[128,1024]{1,0:T(8,128)(2,1)}, bf16[128,1024]{1,0:T(8,128)(2,1)S(1)}, u32[]{:S(2)}, u32[]{:S(2)}) collective-permute-start(bf16[128,1024]{1,0:T(8,128)(2,1)} %bitcast.17), channel_id=1, source_target_pairs={{0,2},{3,1},{4,6},{7,5},{8,10},{11,9},{12,14},{15,13},{16,18},{19,... | collective-permute-start | bytes 786440 | tf_op jit(solution)/shard_map/ppermute | solution.py:173
  42.1 7.1 %collective-permute-start.1 = (bf16[128,1024]{1,0:T(8,128)(2,1)}, bf16[128,1024]{1,0:T(8,128)(2,1)S(1)}, u32[]{:S(2)}, u32[]{:S(2)}) collective-permute-start(bf16[128,1024]{1,0:T(8,128)(2,1)} %bitcast.18), channel_id=1, source_target_pairs={{1,2},{2,1},{5,6},{6,5},{9,10},{10,9},{13,14},{14,13},{17,18},{18,... | collective-permute-start | bytes 786440 | tf_op jit(solution)/shard_map/ppermute | solution.py:172
  48.0 10.8 %collective-permute-start.3 = (bf16[128,1024]{1,0:T(8,128)(2,1)S(1)}, bf16[128,1024]{1,0:T(8,128)(2,1)S(1)}, u32[]{:S(2)}, u32[]{:S(2)}) collective-permute-start(bf16[128,1024]{1,0:T(8,128)(2,1)S(1)} %fusion.6), channel_id=1, source_target_pairs={{0,1},{1,3},{3,2},{2,0},{4,5},{5,7},{7,6},{6,4},{8,9},{9,11},{11,1... | collective-permute-start | bytes 786440 | tf_op jit(solution)/shard_map/ppermute | solution.py:176
